TPU v7x, 256 devices: a whole 4x4x8 slice. The times are simulated.
256 devices in a mesh: fsdp: 32 (over z, y_lo, core), tp: 8 (over x, y_hi).
Axes of the slice: x: 4, y: 4 (y_hi: 2, y_lo: 2; y = y_hi * 2 + y_lo), z: 8, core: 2. Of those that a mesh axis runs over, the one named last changes fastest.
Arguments:
- tokens: bfloat16 [2048, 8192], P('tp', 'fsdp'), may hold values from -6 to 6
- gate_blocks: bfloat16 [256, 22, 128, 128], P(('fsdp', 'tp')), may hold values from -0.109375 to 0.109375
- up_blocks: bfloat16 [256, 22, 128, 128], P(('fsdp', 'tp')), may hold values from -0.109375 to 0.109375
- down_blocks: bfloat16 [256, 22, 128, 128], P(('fsdp', 'tp')), may hold values from -0.0546875 to 0.0546875
- gate_index: int32 [256, 22], P('fsdp'), may hold values from 0 to 63, as said below
- up_index: int32 [256, 22], P('fsdp'), may hold values from 0 to 63, as said below
- down_index: int32 [256, 22], P('fsdp'), may hold values from 0 to 63, as said below
- gate_count: int32 [256], P('fsdp'), may hold values from 14 to 22
- up_count: int32 [256], P('fsdp'), may hold values from 14 to 22
- down_count: int32 [256], P('fsdp'), may hold values from 14 to 22
Outputs:
- mixed: bfloat16 [2048, 8192], P('tp', 'fsdp')
Inputs may be any that keep to these rules, and one draw needn't show every extreme that they name: `gate_index`: in each row the first gate_count entries name the kept row blocks of that block column; the 22 entries of a row are different numbers. `up_index`: in each row the first up_count entries name the kept row blocks of that block column; the 22 entries of a row are different numbers. `down_index`: in each row the first down_count entries name the kept column blocks of that block row; the 22 entries of a row are different numbers.
All inputs are finite; a program needn't handle non-finite values.
Results may differ from a plain program's by a relative error of at most 0.0049.
Values may be sent and summed in bfloat16 or wider, within the bound.
No kernel may reach another device: no remote copies, remote signals or barrier semaphores. Data moves between devices by JAX's collectives and lax.ppermute only.
A program may use at most 192 MiB of HBM per device.

v0:
```python
import jax
import jax.numpy as jnp
from jax import lax
from jax.sharding import PartitionSpec as P


def kept_mask(count_part, slot_num):
    return jnp.arange(slot_num, dtype=jnp.int32)[None, :] < count_part[:, None]


def scatter_rows(partial_out):
    return lax.psum_scatter(partial_out, "fsdp", scatter_dimension=1, tiled=True).astype(
        jnp.bfloat16
    )


def body(
    tokens,
    gate_blocks,
    up_blocks,
    down_blocks,
    gate_index,
    up_index,
    down_index,
    gate_count,
    up_count,
    down_count,
):
    whole = lax.all_gather(tokens, "fsdp", axis=1, tiled=True)
    side_len = gate_blocks.shape[-1]
    row_blocks = whole.shape[1] // side_len
    slot_num = gate_index.shape[1]
    block_ids = jnp.arange(row_blocks, dtype=jnp.int32)

    def project_in(block_set, index_part, count_part):
        col_num = index_part.shape[0]
        live_mask = kept_mask(count_part, slot_num)
        onehot = (
            (index_part[:, :, None] == block_ids[None, None, :]) & live_mask[:, :, None]
        ).astype(jnp.bfloat16)
        panel = jnp.einsum("jki,jkcd->icjd", onehot, block_set, preferred_element_type=jnp.bfloat16)
        panel = panel.reshape(row_blocks * side_len, col_num * side_len)
        return jnp.dot(whole, panel, preferred_element_type=jnp.float32)

    pieces = (
        lax.all_gather(gate_blocks, "tp", axis=0, tiled=True),
        lax.all_gather(up_blocks, "tp", axis=0, tiled=True),
    )
    col_num = pieces[0].shape[0]
    gate_part = project_in(pieces[0], gate_index, gate_count)
    up_part = project_in(pieces[1], up_index, up_count)
    hidden = (jax.nn.silu(gate_part) * up_part).astype(jnp.bfloat16)
    piece = lax.all_gather(down_blocks, "tp", axis=0, tiled=True)
    col_num = piece.shape[0]
    index_part = down_index
    count_part = down_count
    live_mask = kept_mask(count_part, slot_num)
    col_num = piece.shape[0]
    live_mask = kept_mask(count_part, slot_num)
    onehot = ((index_part[:, :, None] == block_ids[None, None, :]) & live_mask[:, :, None]).astype(
        jnp.bfloat16
    )
    panel = jnp.einsum("jki,jkcd->jcid", onehot, piece, preferred_element_type=jnp.bfloat16)
    panel = panel.reshape(col_num * side_len, row_blocks * side_len)
    partial_out = jnp.dot(hidden, panel, preferred_element_type=jnp.float32)
    return scatter_rows(partial_out)


def solution(mesh):
    in_specs = (
        P("tp", "fsdp"),
        P(("fsdp", "tp"), None, None, None),
        P(("fsdp", "tp"), None, None, None),
        P(("fsdp", "tp"), None, None, None),
        P("fsdp", None),
        P("fsdp", None),
        P("fsdp", None),
        P("fsdp"),
        P("fsdp"),
        P("fsdp"),
    )
    out_specs = P("tp", "fsdp")
    return jax.shard_map(body, mesh=mesh, in_specs=in_specs, out_specs=out_specs, check_vma=False)
```

profile of v0, /device:TPU:2, one launch (start us, length us, event | category | flops | bytes accessed | tf_op | source)
XLA Modules:
  0.0 527.5 jit_solution(13812759627836743299)
XLA Ops:
  6.5 0.0 all-gather.5.cloned.1.call-start
  6.5 0.7 all-gather.5.cloned.1.call-update
  7.3 0.0 all-gather.9.cloned.1.call-start
  7.3 0.7 all-gather.9.cloned.1.call-update
  8.0 0.0 all-gather.7.cloned.1.call-start
  8.1 0.7 all-gather.7.cloned.1.call-update
  8.7 0.0 all-gather.11.cloned.1.call-start
  8.8 0.5 all-gather.11.cloned.1.call-update
  9.3 0.0 reduce-scatter.2.cloned.1.call-start
  9.4 0.7 iota_compare_fusion.5
  10.1 0.7 iota_compare_fusion.4
  10.8 0.7 iota_compare_fusion.3
  11.5 89.6 %all-gather.5.cloned.1.call-done = bf16[8,22,128,128]{3,2,1,0:T(8,128)(2,1)} async-done(((bf16[1,22,128,128]{3,2,1,0:T(8,128)(2,1)}), bf16[8,22,128,128]{3,2,1,0:T(8,128)(2,1)}) %all-gather.5.cloned.1.call-update) | async-done | bytes 5767184 | tf_op jit(solution)/shard_map/all_gather | solution.py:46
  101.2 14.3 %convolution_bitcast_fusion.1 = bf16[64,128,8,128]{3,0,1,2:T(8,128)(2,1)} fusion(bf16[8,22,128,128]{3,2,1,0:T(8,128)(2,1)} %all-gather.5.cloned.1.call-done, s32[8,22]{1,0:T(8,128)} %param.14, pred[8,22]{1,0:T(8,128)(4,1)S(1)} %iota_compare_fusion.5), kind=kOutput, calls=%fused_computation.10 | convolution fusion | flops 369121280 | bytes 22545264 | tf_op jit(solution)/shard_map/jki,jkcd->icjd/dot_general | solution.py:41
  115.5 0.0 copy-start
  115.5 19.2 %copy.20 = bf16[64,128,8,128]{3,2,1,0:T(8,128)(2,1)} copy(bf16[64,128,8,128]{3,0,1,2:T(8,128)(2,1)} %convolution_bitcast_fusion.1) | data formatting | bytes 33554432 | tf_op jit(solution)/shard_map/jki,jkcd->icjd/transpose | solution.py:41
  134.7 56.4 %all-gather.9.cloned.1.call-done = bf16[8,22,128,128]{3,2,1,0:T(8,128)(2,1)} async-done(((bf16[1,22,128,128]{3,2,1,0:T(8,128)(2,1)}), bf16[8,22,128,128]{3,2,1,0:T(8,128)(2,1)}) %all-gather.9.cloned.1.call-update) | async-done | bytes 5767184 | tf_op jit(solution)/shard_map/all_gather | solution.py:47
  191.2 0.0 copy-done
  191.2 14.1 %convolution_bitcast_fusion = bf16[64,128,8,128]{3,0,1,2:T(8,128)(2,1)} fusion(bf16[8,22,128,128]{3,2,1,0:T(8,128)(2,1)} %all-gather.9.cloned.1.call-done, s32[8,22]{1,0:T(8,128)S(1)} %copy-done, pred[8,22]{1,0:T(8,128)(4,1)S(1)} %iota_compare_fusion.4), kind=kOutput, calls=%fused_computation.9 | convolution fusion | flops 369121280 | bytes 22545264 | tf_op jit(solution)/shard_map/jki,jkcd->icjd/dot_general | solution.py:41
  205.3 18.7 %copy.22 = bf16[64,128,8,128]{3,2,1,0:T(8,128)(2,1)} copy(bf16[64,128,8,128]{3,0,1,2:T(8,128)(2,1)} %convolution_bitcast_fusion) | data formatting | bytes 33554432 | tf_op jit(solution)/shard_map/jki,jkcd->icjd/transpose | solution.py:41
  224.0 40.3 %all-gather.7.cloned.1.call-done = bf16[256,8192]{1,0:T(8,128)(2,1)} async-done(((bf16[256,256]{1,0:T(8,128)(2,1)}), bf16[256,8192]{1,0:T(8,128)(2,1)}) %all-gather.7.cloned.1.call-update) | async-done | bytes 4194320 | tf_op jit(solution)/shard_map/all_gather | solution.py:29
  264.3 11.8 %fusion.13 = f32[256,1024]{0,1:T(8,128)S(1)} fusion(bf16[256,8192]{1,0:T(8,128)(2,1)} %all-gather.7.cloned.1.call-done, bf16[1024,8,8,128]{3,2,1,0:T(8,128)(2,1)} %bitcast.55), kind=kOutput, calls=%fused_computation.15 | convolution fusion | flops 4294967296 | bytes 22020096 | tf_op jit(solution)/shard_map/dot_general | solution.py:43
  276.1 0.0 copy-done.2
  276.1 0.0 copy-start.1
  276.1 11.4 %fusion.22 = bf16[256,1024]{0,1:T(8,128)(2,1)S(1)} fusion(bf16[256,8192]{1,0:T(8,128)(2,1)S(1)} %copy-done.2, bf16[1024,8,8,128]{3,2,1,0:T(8,128)(2,1)} %bitcast.56, f32[256,1024]{0,1:T(8,128)S(1)} %fusion.13), kind=kOutput, calls=%fused_computation.18 | convolution fusion | flops 4296540160 | bytes 22544384 | tf_op jit(solution)/shard_map/dot_general | solution.py:43
  287.5 66.3 %all-gather.11.cloned.1.call-done = bf16[8,22,128,128]{3,2,1,0:T(8,128)(2,1)} async-done(((bf16[1,22,128,128]{3,2,1,0:T(8,128)(2,1)}), bf16[8,22,128,128]{3,2,1,0:T(8,128)(2,1)}) %all-gather.11.cloned.1.call-update) | async-done | bytes 5767184 | tf_op jit(solution)/shard_map/all_gather | solution.py:53
  353.9 0.0 copy-done.1
  353.9 14.3 %fusion.9 = bf16[8,64,128,128]{3,1,2,0:T(8,128)(2,1)} fusion(bf16[8,22,128,128]{3,2,1,0:T(8,128)(2,1)} %all-gather.11.cloned.1.call-done, s32[8,22]{1,0:T(8,128)S(1)} %copy-done.1, pred[8,22]{1,0:T(8,128)(4,1)S(1)} %iota_compare_fusion.3), kind=kOutput, calls=%fused_computation.11 | convolution fusion | flops 369121280 | bytes 22545264 | tf_op jit(solution)/shard_map/jki,jkcd->jcid/dot_general | solution.py:63
  368.2 20.3 %fusion = f32[256,8192]{1,0:T(8,128)} fusion(bf16[256,1024]{0,1:T(8,128)(2,1)S(1)} %fusion.22, bf16[128,8,64,128]{3,2,1,0:T(8,128)(2,1)} %bitcast.54), kind=kOutput, calls=%fused_computation | convolution fusion | flops 4294967296 | bytes 25690112 | tf_op jit(solution)/shard_map/dot_general | solution.py:65
  388.5 0.0 reduce-scatter.2.cloned.1.call-update
  388.5 130.6 %reduce-scatter.2.cloned.1.call-done = f32[256,256]{1,0:T(8,128)} async-done(((f32[256,8192]{1,0:T(8,128)}), f32[256,256]{1,0:T(8,128)}) %reduce-scatter.2.cloned.1.call-update) | async-done | bytes 262160 | tf_op jit(solution)/shard_map/reduce_scatter | solution.py:12
  519.1 1.6 convert_element_type.10
  (1 shorter events, 0.0 us)
Async XLA Ops:
  6.5 94.6 %all-gather.5.cloned.1.call-start = ((), (), s32[]{:S(2)}) async-start(), calls=%async_computation.1 | async-start | bytes 6488064 | tf_op jit(solution)/shard_map/all_gather | solution.py:46
  7.3 183.9 %all-gather.9.cloned.1.call-start = ((), (), s32[]{:S(2)}) async-start(), calls=%async_computation.3 | async-start | bytes 6488064 | tf_op jit(solution)/shard_map/all_gather | solution.py:47
  8.0 256.3 %all-gather.7.cloned.1.call-start = ((), (), s32[]{:S(2)}) async-start(), calls=%async_computation.2 | async-start | bytes 4325376 | tf_op jit(solution)/shard_map/all_gather | solution.py:29
  8.7 345.1 %all-gather.11.cloned.1.call-start = ((), (), s32[]{:S(2)}) async-start(), calls=%async_computation.4 | async-start | bytes 6488064 | tf_op jit(solution)/shard_map/all_gather | solution.py:53
  9.3 509.8 %reduce-scatter.2.cloned.1.call-start = ((), (), s32[]{:S(2)}) async-start(), calls=%async_computation.5 | async-start | bytes 8650752 | tf_op jit(solution)/shard_map/reduce_scatter | solution.py:12
  115.5 75.7 %copy-start = (s32[8,22]{1,0:T(8,128)S(1)}, s32[8,22]{1,0:T(8,128)}, u32[]{:S(2)}) copy-start(s32[8,22]{1,0:T(8,128)} %param.15) | copy-start | bytes 2116
  264.3 11.8 %copy-start.2 = (bf16[256,8192]{1,0:T(8,128)(2,1)S(1)}, bf16[256,8192]{1,0:T(8,128)(2,1)}, u32[]{:S(2)}) copy-start(bf16[256,8192]{1,0:T(8,128)(2,1)} %all-gather.7.cloned.1.call-done) | copy-start | bytes 12582916
  276.1 77.8 %copy-start.1 = (s32[8,22]{1,0:T(8,128)S(1)}, s32[8,22]{1,0:T(8,128)}, u32[]{:S(2)}) copy-start(s32[8,22]{1,0:T(8,128)} %param.16) | copy-start | bytes 2116
Sparse Core Ops, SparseCore 0:
  9.9 91.1 all-gather.4
  103.8 87.3 all-gather.8
  192.9 71.2 all-gather.6
  266.7 87.0 all-gather.10
  388.6 130.4 reduce-scatter.1
where the time goes:
time: 533 us; the launch traced here: 528 us
  waiting for transfers between devices  386 us (72%)
  matrix products  86.3 us (16%)
  local copies, waits for them, and re-layouts  38 us (7%)
  between operations  13.4 us (3%)
    reduce_scatter x1, waiting for transfers between devices, scatter_rows(): lax.psum_scatter(partial_out, 'fsdp', scatter_dimension=1, tiled=True)  131 us
    all_gather x1, waiting for transfers between devices, body(): lax.all_gather(gate_blocks, 'tp', axis=0, tiled=True)  89.6 us
    all_gather x1, waiting for transfers between devices, body(): piece = lax.all_gather(down_blocks, 'tp', axis=0, tiled=True)  66.3 us
    all_gather x1, waiting for transfers between devices, body(): lax.all_gather(up_blocks, 'tp', axis=0, tiled=True)  56.4 us
    all_gather x1, waiting for transfers between devices, body(): whole = lax.all_gather(tokens, 'fsdp', axis=1, tiled=True)  40.3 us
    transpose x2, local copies, waits for them, and re-layouts, project_in(): jnp.einsum('jki,jkcd->icjd', onehot, block_set, preferred_element_type=jn...  38 us
    dot_general x2, matrix products, project_in(): jnp.einsum('jki,jkcd->icjd', onehot, block_set, preferred_element_type=jn...  28.4 us
    dot_general x2, matrix products, project_in(): return jnp.dot(whole, panel, preferred_element_type=jnp.float32)  23.2 us
  transfers between devices with their start and end apart: 5, of which 5 were waited for; matrix products, arithmetic and copies ran while one was open for 17% of the time, Pallas kernels for 0%

commit v1 on v0

--- a/solution.py
+++ b/solution.py
@@ -2,6 +2,11 @@
 import jax.numpy as jnp
 from jax import lax
 from jax.sharding import PartitionSpec as P
+
+
+def exchange_gather(shard, axis, d):
+    stack = jnp.stack([shard] * lax.axis_size(axis))
+    return jnp.concatenate(lax.all_to_all(stack, axis, 0, 0), axis=d)
 
 
 def kept_mask(count_part, slot_num):
@@ -44,7 +49,7 @@
 
     pieces = (
         lax.all_gather(gate_blocks, "tp", axis=0, tiled=True),
-        lax.all_gather(up_blocks, "tp", axis=0, tiled=True),
+        exchange_gather(up_blocks, "tp", 0),
     )
     col_num = pieces[0].shape[0]
     gate_part = project_in(pieces[0], gate_index, gate_count)

time: 533 us -> 482 us (0.904)
  waiting for transfers between devices: 386 us -> 324 us
  starting transfers between devices: 0.15 us -> 7.69 us
    all_to_all x0 -> x1, waiting for transfers between devices: none -> 93.3 us  [exchange_gather(): return jnp.concatenate(lax.all_to_all(stack, axis, 0, 0), axis=d)]
    all_gather x1, waiting for transfers between devices: 89.6 us -> 0.01 us  [body(): lax.all_gather(gate_blocks, 'tp', axis=0, tiled=True)]
    all_gather x1 -> x0, waiting for transfers between devices: 56.4 us -> none  [body(): lax.all_gather(up_blocks, 'tp', axis=0, tiled=True)]
    all_gather x1, waiting for transfers between devices: 40.3 us -> 31.4 us  [body(): whole = lax.all_gather(tokens, 'fsdp', axis=1, tiled=True)]
    all_to_all x0 -> x1, starting transfers between devices: none -> 7.6 us  [exchange_gather(): return jnp.concatenate(lax.all_to_all(stack, axis, 0, 0), axis=d)]
  transfers between devices with their start and end apart: 5 -> 5, of which waited for: 5 -> 4; matrix products, arithmetic and copies ran while one was open for 17% -> 20% of each run, Pallas kernels for 0% -> 0%
where the time goes in v1:
time: 482 us; the launch traced here: 476 us
  waiting for transfers between devices  324 us (67%)
  matrix products  86.1 us (18%)
  local copies, waits for them, and re-layouts  42.8 us (9%)
  between operations  13.4 us (3%)
  starting transfers between devices  7.69 us (2%)
    reduce_scatter x1, waiting for transfers between devices, scatter_rows(): lax.psum_scatter(partial_out, 'fsdp', scatter_dimension=1, tiled=True)  131 us
    all_to_all x1, waiting for transfers between devices, exchange_gather(): return jnp.concatenate(lax.all_to_all(stack, axis, 0, 0), axis=d)  93.3 us
    all_gather x1, waiting for transfers between devices, body(): piece = lax.all_gather(down_blocks, 'tp', axis=0, tiled=True)  66.5 us
    transpose x2, local copies, waits for them, and re-layouts, project_in(): jnp.einsum('jki,jkcd->icjd', onehot, block_set, preferred_element_type=jn...  37.8 us
    all_gather x1, waiting for transfers between devices, body(): whole = lax.all_gather(tokens, 'fsdp', axis=1, tiled=True)  31.4 us
    dot_general x2, matrix products, project_in(): jnp.einsum('jki,jkcd->icjd', onehot, block_set, preferred_element_type=jn...  28.3 us
    dot_general x2, matrix products, project_in(): return jnp.dot(whole, panel, preferred_element_type=jnp.float32)  23.2 us
    dot_general x1, matrix products, body(): partial_out = jnp.dot(hidden, panel, preferred_element_type=jnp.float32)  20.3 us
  transfers between devices with their start and end apart: 5, of which 4 were waited for; matrix products, arithmetic and copies ran while one was open for 20% of the time, Pallas kernels for 0%

profile of v1, /device:TPU:2, one launch (start us, length us, event | category | flops | bytes accessed | tf_op | source)
XLA Modules:
  0.0 476.0 jit_solution(15092943959855379080)
XLA Ops:
  6.5 0.0 all-gather.4.cloned.1.call-start
  6.5 0.7 all-gather.4.cloned.1.call-update
  7.3 0.0 all-gather.6.cloned.1.call-start
  7.3 0.7 all-gather.6.cloned.1.call-update
  8.0 5.1 %stack.2 = bf16[8,1,22,128,128]{4,3,2,1,0:T(8,128)(2,1)} broadcast(bf16[22,128,128]{2,1,0:T(8,128)(2,1)} %bitcast.61), dimensions={2,3,4} | broadcast | bytes 6488064 | tf_op jit(solution)/shard_map/stack | solution.py:8
  13.1 7.6 %all-to-all-start = ((bf16[8,1,22,128,128]{4,3,2,1,0:T(8,128)(2,1)}), bf16[8,1,22,128,128]{4,3,2,1,0:T(8,128)(2,1)}, u32[]{:S(2)}, u32[]{:S(2)}) async-start(bf16[8,1,22,128,128]{4,3,2,1,0:T(8,128)(2,1)} %stack.2), calls=%async_computation | async-start | bytes 11534336 | tf_op jit(solution)/shard_map/all_to_all | solution.py:9
  20.7 0.0 all-gather.8.cloned.1.call-start
  20.7 0.7 all-gather.8.cloned.1.call-update
  21.4 0.0 reduce-scatter.2.cloned.1.call-start
  21.5 0.0 copy-done.4
  21.5 0.1 iota_compare_fusion.5
  21.5 0.0 copy-done.5
  21.5 0.1 iota_compare_fusion.4
  21.6 0.0 copy-done.6
  21.6 0.1 iota_compare_fusion.3
  21.7 93.3 %all-to-all-done = bf16[8,1,22,128,128]{4,3,2,1,0:T(8,128)(2,1)} async-done(((bf16[8,1,22,128,128]{4,3,2,1,0:T(8,128)(2,1)}), bf16[8,1,22,128,128]{4,3,2,1,0:T(8,128)(2,1)}, u32[]{:S(2)}, u32[]{:S(2)}) %all-to-all-start) | async-done | bytes 5767200 | tf_op jit(solution)/shard_map/all_to_all | solution.py:9
  115.0 0.0 copy-done
  115.0 14.2 %convolution_bitcast_fusion = bf16[64,128,8,128]{3,0,1,2:T(8,128)(2,1)} fusion(bf16[8,1,22,128,128]{4,3,2,1,0:T(8,128)(2,1)} %all-to-all-done, s32[8,22]{1,0:T(8,128)S(1)} %copy-done, pred[8,22]{1,0:T(8,128)(4,1)S(1)} %iota_compare_fusion.4), kind=kOutput, calls=%fused_computation.9 | convolution fusion | flops 369121280 | bytes 22545264 | tf_op jit(solution)/shard_map/jki,jkcd->icjd/dot_general | solution.py:46
  129.2 19.0 %copy.22 = bf16[64,128,8,128]{3,2,1,0:T(8,128)(2,1)} copy(bf16[64,128,8,128]{3,0,1,2:T(8,128)(2,1)} %convolution_bitcast_fusion) | data formatting | bytes 33554432 | tf_op jit(solution)/shard_map/jki,jkcd->icjd/transpose | solution.py:46
  148.2 0.0 copy-done.1
  148.2 14.1 %convolution_bitcast_fusion.1 = bf16[64,128,8,128]{3,0,1,2:T(8,128)(2,1)} fusion(bf16[8,22,128,128]{3,2,1,0:T(8,128)(2,1)} %all-gather.4.cloned.1.call-done, s32[8,22]{1,0:T(8,128)S(1)} %copy-done.1, pred[8,22]{1,0:T(8,128)(4,1)S(1)} %iota_compare_fusion.5), kind=kOutput, calls=%fused_computation.10 | convolution fusion | flops 369121280 | bytes 22545264 | tf_op jit(solution)/shard_map/jki,jkcd->icjd/dot_general | solution.py:46
  162.3 18.7 %copy.20 = bf16[64,128,8,128]{3,2,1,0:T(8,128)(2,1)} copy(bf16[64,128,8,128]{3,0,1,2:T(8,128)(2,1)} %convolution_bitcast_fusion.1) | data formatting | bytes 33554432 | tf_op jit(solution)/shard_map/jki,jkcd->icjd/transpose | solution.py:46
  181.1 31.4 %all-gather.6.cloned.1.call-done = bf16[256,8192]{1,0:T(8,128)(2,1)} async-done(((bf16[256,256]{1,0:T(8,128)(2,1)}), bf16[256,8192]{1,0:T(8,128)(2,1)}) %all-gather.6.cloned.1.call-update) | async-done | bytes 4194320 | tf_op jit(solution)/shard_map/all_gather | solution.py:34
  212.5 11.8 %fusion.14 = f32[256,1024]{0,1:T(8,128)S(1)} fusion(bf16[256,8192]{1,0:T(8,128)(2,1)} %all-gather.6.cloned.1.call-done, bf16[1024,8,8,128]{3,2,1,0:T(8,128)(2,1)} %bitcast.60), kind=kOutput, calls=%fused_computation.16 | convolution fusion | flops 4294967296 | bytes 22020096 | tf_op jit(solution)/shard_map/dot_general | solution.py:48
  224.3 0.0 copy-start.2
  224.3 11.4 %fusion.23 = bf16[256,1024]{0,1:T(8,128)(2,1)S(1)} fusion(bf16[256,8192]{1,0:T(8,128)(2,1)S(1)} %copy-done.3, bf16[1024,8,8,128]{3,2,1,0:T(8,128)(2,1)} %bitcast.59, f32[256,1024]{0,1:T(8,128)S(1)} %fusion.14), kind=kOutput, calls=%fused_computation.19 | convolution fusion | flops 4296540160 | bytes 22544384 | tf_op jit(solution)/shard_map/dot_general | solution.py:48
  235.8 66.5 %all-gather.8.cloned.1.call-done = bf16[8,22,128,128]{3,2,1,0:T(8,128)(2,1)} async-done(((bf16[1,22,128,128]{3,2,1,0:T(8,128)(2,1)}), bf16[8,22,128,128]{3,2,1,0:T(8,128)(2,1)}) %all-gather.8.cloned.1.call-update) | async-done | bytes 5767184 | tf_op jit(solution)/shard_map/all_gather | solution.py:58
  302.2 14.3 %fusion.10 = bf16[8,64,128,128]{3,1,2,0:T(8,128)(2,1)} fusion(bf16[8,22,128,128]{3,2,1,0:T(8,128)(2,1)} %all-gather.8.cloned.1.call-done, s32[8,22]{1,0:T(8,128)S(1)} %copy-done.2, pred[8,22]{1,0:T(8,128)(4,1)S(1)} %iota_compare_fusion.3), kind=kOutput, calls=%fused_computation.12 | convolution fusion | flops 369121280 | bytes 22545264 | tf_op jit(solution)/shard_map/jki,jkcd->jcid/dot_general | solution.py:68
  316.6 20.3 %fusion = f32[256,8192]{1,0:T(8,128)} fusion(bf16[256,1024]{0,1:T(8,128)(2,1)S(1)} %fusion.23, bf16[128,8,64,128]{3,2,1,0:T(8,128)(2,1)} %bitcast.58), kind=kOutput, calls=%fused_computation | convolution fusion | flops 4294967296 | bytes 25690112 | tf_op jit(solution)/shard_map/dot_general | solution.py:70
  336.9 0.0 reduce-scatter.2.cloned.1.call-update
  336.9 130.7 %reduce-scatter.2.cloned.1.call-done = f32[256,256]{1,0:T(8,128)} async-done(((f32[256,8192]{1,0:T(8,128)}), f32[256,256]{1,0:T(8,128)}) %reduce-scatter.2.cloned.1.call-update) | async-done | bytes 262160 | tf_op jit(solution)/shard_map/reduce_scatter | solution.py:17
  467.6 1.6 convert_element_type.10
  (9 shorter events, 0.0 us)
Async XLA Ops:
  6.5 141.7 %all-gather.4.cloned.1.call-start = ((), (), s32[]{:S(2)}) async-start(), calls=%async_computation.2 | async-start | bytes 6488064 | tf_op jit(solution)/shard_map/all_gather | solution.py:51
  7.3 205.3 %all-gather.6.cloned.1.call-start = ((), (), s32[]{:S(2)}) async-start(), calls=%async_computation.3 | async-start | bytes 4325376 | tf_op jit(solution)/shard_map/all_gather | solution.py:34
  13.1 8.4 %copy-start.4 = (s32[8]{0:T(128)S(1)}, s32[8]{0:T(128)}, u32[]{:S(2)}) copy-start(s32[8]{0:T(128)} %param.17) | copy-start | bytes 100
  13.1 8.5 %copy-start.5 = (s32[8]{0:T(128)S(1)}, s32[8]{0:T(128)}, u32[]{:S(2)}) copy-start(s32[8]{0:T(128)} %param.18) | copy-start | bytes 100
  13.1 8.5 %copy-start.6 = (s32[8]{0:T(128)S(1)}, s32[8]{0:T(128)}, u32[]{:S(2)}) copy-start(s32[8]{0:T(128)} %param.19) | copy-start | bytes 100
  13.1 101.9 %copy-start = (s32[8,22]{1,0:T(8,128)S(1)}, s32[8,22]{1,0:T(8,128)}, u32[]{:S(2)}) copy-start(s32[8,22]{1,0:T(8,128)} %param.15) | copy-start | bytes 2116
  13.1 101.9 %all-to-all-start = ((bf16[8,1,22,128,128]{4,3,2,1,0:T(8,128)(2,1)}), bf16[8,1,22,128,128]{4,3,2,1,0:T(8,128)(2,1)}, u32[]{:S(2)}, u32[]{:S(2)}) async-start(bf16[8,1,22,128,128]{4,3,2,1,0:T(8,128)(2,1)} %stack.2), calls=%async_computation | async-start | bytes 11534336 | tf_op jit(solution)/shard_map/all_to_all | solution.py:9
  20.7 281.6 %all-gather.8.cloned.1.call-start = ((), (), s32[]{:S(2)}) async-start(), calls=%async_computation.4 | async-start | bytes 6488064 | tf_op jit(solution)/shard_map/all_gather | solution.py:58
  21.4 446.2 %reduce-scatter.2.cloned.1.call-start = ((), (), s32[]{:S(2)}) async-start(), calls=%async_computation.5 | async-start | bytes 8650752 | tf_op jit(solution)/shard_map/reduce_scatter | solution.py:17
  129.2 19.0 %copy-start.1 = (s32[8,22]{1,0:T(8,128)S(1)}, s32[8,22]{1,0:T(8,128)}, u32[]{:S(2)}) copy-start(s32[8,22]{1,0:T(8,128)} %param.14) | copy-start | bytes 2116
  212.5 11.8 %copy-start.3 = (bf16[256,8192]{1,0:T(8,128)(2,1)S(1)}, bf16[256,8192]{1,0:T(8,128)(2,1)}, u32[]{:S(2)}) copy-start(bf16[256,8192]{1,0:T(8,128)(2,1)} %all-gather.6.cloned.1.call-done) | copy-start | bytes 12582916
  224.3 77.9 %copy-start.2 = (s32[8,22]{1,0:T(8,128)S(1)}, s32[8,22]{1,0:T(8,128)}, u32[]{:S(2)}) copy-start(s32[8,22]{1,0:T(8,128)} %param.16) | copy-start | bytes 2116
Sparse Core Ops, SparseCore 0:
  9.9 129.7 all-gather.3
  141.5 70.9 all-gather.5
  215.1 87.0 all-gather.7
  337.0 130.4 reduce-scatter.1
